TPU v7x, 32 devices: a whole 2x2x4 slice. The times are simulated.
32 devices in a mesh: dp: 4 (over y, x), fsdp: 8 (over z, core).
Axes of the slice: x: 2, y: 2, z: 4, core: 2. Of those that a mesh axis runs over, the one named last changes fastest.
Arguments:
- hidden: bfloat16 [2, 4608, 4096], P(None, ('dp', 'fsdp')), may hold values from -120 to 120
- cotangent: bfloat16 [2, 4608, 1024], P(None, ('dp', 'fsdp')), may hold values from -6 to 6
- proj_weight: bfloat16 [2, 4096, 1024], P(None, 'fsdp'), may hold values from -3 to 3
- norm_gain: float32 [2, 4096], replicated, may hold values from 0.1 to 1.9
- prev_factor: bfloat16 [2, 512, 128], replicated, may hold values from -0.25 to 0.25
- factor_ranks: int32 [2, 2], replicated, may hold values from 4 to 64, as said below
- layer_order: int32 [2], replicated, may hold values from 0 to 1, each once
Outputs:
- hidden_grad: bfloat16 [4608, 4096], P(('dp', 'fsdp'))
- basis_factor: float32 [2, 4096, 128], P(None, 'fsdp')
Inputs may be any that keep to these rules, and one draw needn't show every extreme that they name: `factor_ranks`: every draw holds a rank equal to 64 and a rank equal to 4.
All inputs are finite; a program needn't handle non-finite values.
Results may differ from a plain program's by a relative error of at most 0.0056.
Values may be sent and summed in bfloat16 or wider, within the bound.
A program may use at most 64 MiB of HBM per device.

v0:
```python
import math
import jax
import jax.numpy as jnp
from jax import lax
from jax.sharding import PartitionSpec as P

D = 4096


def normalize(hidden_rows, gain_row):
    wide_rows = hidden_rows.astype(jnp.float32)
    inverse = lax.rsqrt(jnp.mean(wide_rows * wide_rows, axis=1, keepdims=True) + 1e-05)
    normed = (wide_rows * inverse * gain_row[None, :]).astype(jnp.bfloat16)
    return (inverse, normed)


def masked_factors(factors, rank_pair):
    rank_cols = factors.shape[1] // 2
    position = jnp.arange(2 * rank_cols)
    column = position % rank_cols
    column_limit = jnp.where(position < rank_cols, rank_pair[0], rank_pair[1])
    return jnp.where((column < column_limit)[None, :], factors, jnp.zeros_like(factors))


def project(grad_rows, kept_factor):
    head_cols = grad_rows.shape[1] // 2
    rank_cols = kept_factor.shape[1] // 2
    keys_part = jnp.dot(
        grad_rows[:, :head_cols], kept_factor[:, :rank_cols], preferred_element_type=jnp.float32
    )
    values_part = jnp.dot(
        grad_rows[:, head_cols:], kept_factor[:, rank_cols:], preferred_element_type=jnp.float32
    )
    return jnp.concatenate([keys_part, values_part], axis=1).astype(jnp.bfloat16)


def gram_pair(factor_shard):
    row_count = factor_shard.shape[0]
    rank_cols = factor_shard.shape[1] // 2
    paired = factor_shard.reshape(row_count, 2, rank_cols)
    return jnp.einsum(
        "rmi,rmj->mij",
        paired,
        paired,
        precision=lax.Precision.HIGHEST,
        preferred_element_type=jnp.float32,
    )


def orthonormal(factor_shard, gram_totals, rank_pair):
    rank_cols = factor_shard.shape[1] // 2
    column = jnp.arange(rank_cols)
    pieces = []
    for member in range(2):
        block_cols = factor_shard[:, member * rank_cols : (member + 1) * rank_cols]
        padded = gram_totals[member] + jnp.diag((column >= rank_pair[member]).astype(jnp.float32))
        lower_factor = jnp.linalg.cholesky(padded)
        pieces.append(
            lax.linalg.triangular_solve(
                lower_factor, block_cols, left_side=False, lower=True, transpose_a=True
            )
        )
    return math.sqrt(D) * jnp.concatenate(pieces, axis=1)


def body(hidden, cotangent, proj_weight, norm_gain, prev_factor, factor_ranks, layer_order):
    layer_count = hidden.shape[0]
    top_slot = layer_order[0]
    inverses = []
    shards = []
    basis_list = []
    for slot_index in range(layer_count):
        inverse, normed = normalize(hidden[slot_index], norm_gain[slot_index])
        inverses.append(inverse)
        kept_factor = masked_factors(prev_factor[slot_index], factor_ranks[slot_index])
        projected = project(cotangent[slot_index], kept_factor)
        local_rows = lax.psum_scatter(
            lax.dot_general(
                normed, projected, (((0,), (0,)), ((), ())), preferred_element_type=jnp.float32
            ),
            "fsdp",
            scatter_dimension=0,
            tiled=True,
        )
        factor_shard = lax.psum(local_rows, "dp")
        shards.append(factor_shard)
    stacked = jnp.stack([gram_pair(factor_shard) for factor_shard in shards])
    all_grams = lax.psum(stacked, "fsdp")
    basis_list = [
        orthonormal(shards[slot_index], all_grams[slot_index], factor_ranks[slot_index])
        for slot_index in range(layer_count)
    ]
    top_grads = lax.dynamic_index_in_dim(cotangent, top_slot, 0, keepdims=False)
    top_weight = lax.dynamic_index_in_dim(proj_weight, top_slot, 0, keepdims=False)
    input_grad = lax.dot_general(
        top_grads,
        lax.all_gather(top_weight, "fsdp", axis=0, tiled=True),
        (((1,), (1,)), ((), ())),
        preferred_element_type=jnp.float32,
    )
    top_inverse = lax.dynamic_index_in_dim(jnp.stack(inverses), top_slot, 0, keepdims=False)
    top_gain = lax.dynamic_index_in_dim(norm_gain, top_slot, 0, keepdims=False)
    top_hidden = lax.dynamic_index_in_dim(hidden, top_slot, 0, keepdims=False).astype(jnp.float32)
    scaled = input_grad * top_gain[None, :]
    unit_rows = top_hidden * top_inverse
    inner_mean = jnp.mean(scaled * unit_rows, axis=1, keepdims=True)
    hidden_grad = (top_inverse * (scaled - unit_rows * inner_mean)).astype(jnp.bfloat16)
    return (hidden_grad, jnp.stack(basis_list))


def solution(mesh):
    in_specs = (
        P(None, ("dp", "fsdp"), None),
        P(None, ("dp", "fsdp"), None),
        P(None, "fsdp", None),
        P(),
        P(),
        P(),
        P(),
    )
    out_specs = (P(("dp", "fsdp"), None), P(None, "fsdp", None))
    return jax.shard_map(body, mesh=mesh, in_specs=in_specs, out_specs=out_specs, check_vma=False)
```

profile of v0, /device:TPU:0, one launch (start us, length us, event | category | flops | bytes accessed | tf_op | source)
XLA Modules:
  0.0 299.6 jit_solution(16446004569142756650)
XLA Ops:
  7.2 1.2 slice_bitcast_fusion.1
  8.5 1.4 fusion.76
  9.9 2.4 fusion.71
  13.9 2.2 fusion.8
  16.2 3.5 %fusion.17 = f32[4096,128]{1,0:T(8,128)} fusion(f32[4096]{0:T(1024)S(1)} %bitcast.139, f32[144]{0:T(256)S(1)} %add_rsqrt_fusion, bf16[2,144,4096]{2,1,0:T(8,128)(2,1)} %param.10, bf16[144,64]{0,1:T(8,128)(2,1)S(1)} %fusion.30, bf16[144,64]{0,1:T(8,128)(2,1)S(1)} %fusion.29), kind=kOutput, calls=%fused_computation.20 | convolution fusion | flops 153427968 | bytes 3330624 | tf_op jit(solution)/shard_map/dot_general | solution.py:78
  20.3 3.5 %fusion.19 = f32[4096,128]{1,0:T(8,128)} fusion(f32[4096]{0:T(1024)S(1)} %bitcast.138, f32[144]{0:T(256)S(1)} %add_rsqrt_fusion.1, bf16[2,144,4096]{2,1,0:T(8,128)(2,1)} %param.10, bf16[144,64]{0,1:T(8,128)(2,1)S(1)} %fusion.28, bf16[144,64]{0,1:T(8,128)(2,1)S(1)} %fusion.27), kind=kOutput, calls=%fused_computation.21 | convolution fusion | flops 153427968 | bytes 3330624 | tf_op jit(solution)/shard_map/dot_general | solution.py:78
  23.8 34.8 %reduce-scatter.5.cloned.1.call-done = f32[512,128]{1,0:T(8,128)} async-done(((f32[4096,128]{1,0:T(8,128)}), f32[512,128]{1,0:T(8,128)}) %reduce-scatter.5.cloned.1.call-update) | async-done | bytes 262160 | tf_op jit(solution)/shard_map/reduce_scatter | solution.py:77
  58.6 37.0 %reduce-scatter.3.cloned.1.call-done = f32[512,128]{1,0:T(8,128)} async-done(((f32[4096,128]{1,0:T(8,128)}), f32[512,128]{1,0:T(8,128)}) %reduce-scatter.3.cloned.1.call-update) | async-done | bytes 262160 | tf_op jit(solution)/shard_map/reduce_scatter | solution.py:77
  95.6 47.0 %all-reduce.6.cloned.1.call-done = (f32[512,128]{1,0:T(8,128)}, f32[512,128]{1,0:T(8,128)}) async-done(((f32[512,128]{1,0:T(8,128)}, f32[512,128]{1,0:T(8,128)}), (f32[512,128]{1,0:T(8,128)}, f32[512,128]{1,0:T(8,128)})) %all-reduce.6.cloned.1.call-update) | async-done | bytes 524304 | tf_op jit(solution)/shard_map/psum | solution.py:85
  144.1 1.1 copy.20
  147.6 1.3 compare_convert_fusion.2
  148.9 1.2 compare_convert_fusion
  150.1 51.2 %all-reduce.4.cloned.1.call-done = f32[2,2,64,64]{2,3,1,0:T(8,128)} async-done(((f32[2,2,64,64]{2,3,1,0:T(8,128)}), f32[2,2,64,64]{2,3,1,0:T(8,128)}) %all-reduce.4.cloned.1.call-update) | async-done | bytes 65552 | tf_op jit(solution)/shard_map/psum | solution.py:88
  202.3 5.8 %cholesky.107 = f32[64,64]{1,0:T(8,128)S(1)} custom-call(f32[64,64]{1,0:T(8,128)S(1)} %fusion.62), custom_call_target="Cholesky" | custom-call | tf_op jit(solution)/shard_map/jit(cholesky)/cholesky | solution.py:57
  209.5 4.9 %custom-call.11 = f32[1,64,64]{1,2,0:T(8,128)S(1)} custom-call(f32[1,64,64]{2,1,0:T(8,128)S(1)} %fusion.56), custom_call_target="InvertDiagBlocksLowerTriangular" | custom-call | tf_op jit(solution)/shard_map/triangular_solve/custom-call.0 | solution.py:59
  214.5 5.8 %cholesky.96 = f32[64,64]{1,0:T(8,128)S(1)} custom-call(f32[64,64]{1,0:T(8,128)S(1)} %fusion.64), custom_call_target="Cholesky" | custom-call | tf_op jit(solution)/shard_map/jit(cholesky)/cholesky | solution.py:57
  221.7 4.9 %custom-call.10 = f32[1,64,64]{1,2,0:T(8,128)S(1)} custom-call(f32[1,64,64]{2,1,0:T(8,128)S(1)} %fusion.55), custom_call_target="InvertDiagBlocksLowerTriangular" | custom-call | tf_op jit(solution)/shard_map/triangular_solve/custom-call.0 | solution.py:59
  226.7 5.8 %cholesky.85 = f32[64,64]{1,0:T(8,128)S(1)} custom-call(f32[64,64]{1,0:T(8,128)S(1)} %fusion.66), custom_call_target="Cholesky" | custom-call | tf_op jit(solution)/shard_map/jit(cholesky)/cholesky | solution.py:57
  233.9 4.9 %custom-call.9 = f32[1,64,64]{1,2,0:T(8,128)S(1)} custom-call(f32[1,64,64]{2,1,0:T(8,128)S(1)} %fusion.54), custom_call_target="InvertDiagBlocksLowerTriangular" | custom-call | tf_op jit(solution)/shard_map/triangular_solve/custom-call.0 | solution.py:59
  238.9 5.8 %cholesky.74 = f32[64,64]{1,0:T(8,128)S(1)} custom-call(f32[64,64]{1,0:T(8,128)S(1)} %fusion.68), custom_call_target="Cholesky" | custom-call | tf_op jit(solution)/shard_map/jit(cholesky)/cholesky | solution.py:57
  246.1 4.9 %custom-call.8 = f32[1,64,64]{1,2,0:T(8,128)S(1)} custom-call(f32[1,64,64]{2,1,0:T(8,128)S(1)} %fusion.53), custom_call_target="InvertDiagBlocksLowerTriangular" | custom-call | tf_op jit(solution)/shard_map/triangular_solve/custom-call.0 | solution.py:59
  254.0 30.6 %all-gather.3.cloned.1.call-done = bf16[1,4096,1024]{2,1,0:T(8,128)(2,1)} async-done(((bf16[1,512,1024]{2,1,0:T(8,128)(2,1)}), bf16[1,4096,1024]{2,1,0:T(8,128)(2,1)}) %all-gather.3.cloned.1.call-update) | async-done | bytes 8388624 | tf_op jit(solution)/shard_map/all_gather | solution.py:97
  284.6 6.9 %fusion.13 = (f32[144]{0:T(256)S(1)}, f32[144,4096]{1,0:T(8,128)S(1)}) fusion(f32[144]{0:T(256)S(1)} %bitcast.141, bf16[2,144,4096]{2,1,0:T(8,128)(2,1)} %param.10, s32[]{:T(128)S(6)} %select_n.69, f32[4096]{0:T(1024)S(1)} %bitcast.140, bf16[1,4096,1024]{2,1,0:T(8,128)(2,1)} %all-gather.3.cloned.1.call-done, bf16[2,144,1024]{2,1,0:T(8,128)(2,1)S(1)} %copy-done.4), kind=kOutput, calls=%fused_computation.16 | convolution fusion | flops 1210908544 | bytes 12241472 | tf_op jit(solution)/shard_map/dot_general | solution.py:95
  291.5 1.6 fusion.16
  (68 shorter events, 15.7 us)
Async XLA Ops:
  7.2 139.4 %copy-start = (bf16[2,512,1024]{2,1,0:T(8,128)(2,1)S(1)}, bf16[2,512,1024]{2,1,0:T(8,128)(2,1)}, u32[]{:S(2)}) copy-start(bf16[2,512,1024]{2,1,0:T(8,128)(2,1)} %param.12) | copy-start | bytes 6291460
  7.2 6.7 %copy-start.6 = (s32[2]{0:T(128)S(1)}, s32[2]{0:T(128)}, u32[]{:S(2)}) copy-start(s32[2]{0:T(128)} %param.16) | copy-start | bytes 28
  7.2 9.0 %copy-start.5 = (f32[2,4096]{1,0:T(2,128)S(1)}, f32[2,4096]{1,0:T(2,128)}, u32[]{:S(2)}) copy-start(f32[2,4096]{1,0:T(2,128)} %param.13) | copy-start | bytes 98308
  7.2 51.4 %reduce-scatter.5.cloned.1.call-start = ((), (), s32[]{:S(2)}) async-start(), calls=%async_computation.3 | async-start | bytes 2359296 | tf_op jit(solution)/shard_map/reduce_scatter | solution.py:77
  19.7 75.8 %reduce-scatter.3.cloned.1.call-start = ((), (), s32[]{:S(2)}) async-start(), calls=%async_computation.2 | async-start | bytes 2359296 | tf_op jit(solution)/shard_map/reduce_scatter | solution.py:77
  23.8 118.9 %all-reduce.6.cloned.1.call-start = ((), (), s32[]{:S(2)}) async-start(), calls=%async_computation.6 | async-start | bytes 1048576 | tf_op jit(solution)/shard_map/psum | solution.py:85
  95.6 105.8 %all-reduce.4.cloned.1.call-start = ((), (), s32[]{:S(2)}) async-start(), calls=%async_computation.4 | async-start | bytes 262144 | tf_op jit(solution)/shard_map/psum | solution.py:88
  146.3 104.7 %copy-start.3 = (f32[512,128]{1,0:T(8,128)S(1)}, f32[512,128]{1,0:T(8,128)}, u32[]{:S(2)}) copy-start(f32[512,128]{1,0:T(8,128)} %get-tuple-element.10) | copy-start | bytes 786436
  146.3 138.2 %all-gather.3.cloned.1.call-start = ((), (), s32[]{:S(2)}) async-start(), calls=%async_computation.5 | async-start | bytes 9437184 | tf_op jit(solution)/shard_map/all_gather | solution.py:97
  147.6 104.4 %copy-start.2 = (f32[512,128]{1,0:T(8,128)S(1)}, f32[512,128]{1,0:T(8,128)}, u32[]{:S(2)}) copy-start(f32[512,128]{1,0:T(8,128)} %get-tuple-element.11) | copy-start | bytes 786436
  251.0 33.6 %copy-start.4 = (bf16[2,144,1024]{2,1,0:T(8,128)(2,1)S(1)}, bf16[2,144,1024]{2,1,0:T(8,128)(2,1)}, u32[]{:S(2)}) copy-start(bf16[2,144,1024]{2,1,0:T(8,128)(2,1)} %param.11) | copy-start | bytes 1769476
  284.6 6.9 %copy-start.1 = (bf16[2,144,4096]{2,1,0:T(8,128)(2,1)S(1)}, bf16[2,144,4096]{2,1,0:T(8,128)(2,1)}, u32[]{:S(2)}) copy-start(bf16[2,144,4096]{2,1,0:T(8,128)(2,1)} %param.10) | copy-start | bytes 7077892
Sparse Core Ops, SparseCore 0:
  19.9 38.7 reduce-scatter.4
  60.9 34.6 reduce-scatter.2
  98.6 44.0 all-reduce.5
  146.4 54.8 all-reduce.3
  203.4 81.1 all-gather.2
where the time goes:
time: 300 us
  waiting for transfers between devices  201 us (67%)
  other arithmetic  59.6 us (20%)
  matrix products  17.6 us (6%)
  between operations  14.2 us (5%)
  local copies, waits for them, and re-layouts  7.26 us (2%)
    reduce_scatter x2, waiting for transfers between devices, body(): lax.psum_scatter(lax.dot_general(normed, projected, (((0,), (0,)), ((), (...  71.7 us
    psum x1, waiting for transfers between devices, body(): all_grams = lax.psum(stacked, 'fsdp')  51.2 us
    psum x1, waiting for transfers between devices, body(): factor_shard = lax.psum(local_rows, 'dp')  47 us
    all_gather x1, waiting for transfers between devices, body(): lax.all_gather(top_weight, 'fsdp', axis=0, tiled=True)  30.6 us
    another operation x12, other arithmetic, orthonormal(): lower_factor = jnp.linalg.cholesky(padded)  26.1 us
    another operation x8, other arithmetic, orthonormal(): lax.linalg.triangular_solve(lower_factor, block_cols, left_side=False, lo...  22.2 us
    dot_general x2, matrix products, body(): lax.dot_general(normed, projected, (((0,), (0,)), ((), ())), preferred_el...  6.96 us
    dot_general x1, matrix products, body(): lax.dot_general(top_grads, lax.all_gather(top_weight, 'fsdp', axis=0, til...  6.9 us
  transfers between devices with their start and end apart: 5, of which 5 were waited for; matrix products, arithmetic and copies ran while one was open for 20% of the time, Pallas kernels for 0%

commit v1 on v0

--- a/solution.py
+++ b/solution.py
@@ -85,7 +85,16 @@
         factor_shard = lax.psum(local_rows, "dp")
         shards.append(factor_shard)
     stacked = jnp.stack([gram_pair(factor_shard) for factor_shard in shards])
-    all_grams = lax.psum(stacked, "fsdp")
+
+    def expand_floor(message):
+        ndev = lax.axis_size("fsdp")
+        low = lambda state_next: [(dd, dd ^ state_next) for dd in range(ndev)]
+        t1 = message
+        for hop_no in range(ndev.bit_length() - 1):
+            t1 = t1 + lax.ppermute(t1, "fsdp", low(1 << hop_no))
+        return t1
+
+    all_grams = expand_floor(stacked)
     basis_list = [
         orthonormal(shards[slot_index], all_grams[slot_index], factor_ranks[slot_index])
         for slot_index in range(layer_count)

time: 300 us -> 247 us (0.82)
  waiting for transfers between devices: 201 us -> 144 us
  starting transfers between devices: 0.38 us -> 4.45 us
    psum x1 -> x0, waiting for transfers between devices: 51.2 us -> none  [body(): all_grams = lax.psum(stacked, 'fsdp')]
    all_gather x1, waiting for transfers between devices: 30.6 us -> 9.06 us  [body(): lax.all_gather(top_weight, 'fsdp', axis=0, tiled=True)]
    ppermute x0 -> x3, waiting for transfers between devices: none -> 17.9 us  [expand_floor(): t1 = t1 + lax.ppermute(t1, 'fsdp', low(1 << hop_no))]
    ppermute x0 -> x3, starting transfers between devices: none -> 4.1 us  [expand_floor(): t1 = t1 + lax.ppermute(t1, 'fsdp', low(1 << hop_no))]
  transfers between devices with their start and end apart: 5 -> 7, of which waited for: 5 -> 7; matrix products, arithmetic and copies ran while one was open for 20% -> 25% of each run, Pallas kernels for 0% -> 0%
where the time goes in v1:
time: 247 us
  waiting for transfers between devices  144 us (58%)
  other arithmetic  58.4 us (24%)
  matrix products  17.6 us (7%)
  between operations  14.2 us (6%)
  local copies, waits for them, and re-layouts  7.37 us (3%)
  starting transfers between devices  4.45 us (2%)
    reduce_scatter x2, waiting for transfers between devices, body(): lax.psum_scatter(lax.dot_general(normed, projected, (((0,), (0,)), ((), (...  71.7 us
    psum x1, waiting for transfers between devices, body(): factor_shard = lax.psum(local_rows, 'dp')  45.8 us
    another operation x12, other arithmetic, orthonormal(): lower_factor = jnp.linalg.cholesky(padded)  26.1 us
    another operation x8, other arithmetic, orthonormal(): lax.linalg.triangular_solve(lower_factor, block_cols, left_side=False, lo...  22.2 us
    ppermute x3, waiting for transfers between devices, expand_floor(): t1 = t1 + lax.ppermute(t1, 'fsdp', low(1 << hop_no))  17.9 us
    all_gather x1, waiting for transfers between devices, body(): lax.all_gather(top_weight, 'fsdp', axis=0, tiled=True)  9.06 us
    dot_general x2, matrix products, body(): lax.dot_general(normed, projected, (((0,), (0,)), ((), ())), preferred_el...  6.96 us
    dot_general x1, matrix products, body(): lax.dot_general(top_grads, lax.all_gather(top_weight, 'fsdp', axis=0, til...  6.9 us
  transfers between devices with their start and end apart: 7, of which 7 were waited for; matrix products, arithmetic and copies ran while one was open for 25% of the time, Pallas kernels for 0%

profile of v1, /device:TPU:0, one launch (start us, length us, event | category | flops | bytes accessed | tf_op | source)
XLA Modules:
  0.0 246.5 jit_solution(13303343819824546037)
XLA Ops:
  8.5 1.5 fusion.77
  10.0 2.6 %fusion.71 = (pred[128]{0:T(512)(128)(4,1)S(1)}, pred[128]{0:T(512)(128)(4,1)S(1)}) fusion(s32[]{:T(128)} %bitcast.13, s32[]{:T(128)} %bitcast.12, s32[]{:T(128)} %bitcast.23, s32[]{:T(128)} %bitcast.22), kind=kLoop, calls=%fused_computation.126 | loop fusion | flops 1408 | bytes 272 | tf_op jit(solution)/shard_map/lt | solution.py:22
  14.1 2.2 fusion.8
  16.4 3.5 %fusion.17 = f32[4096,128]{1,0:T(8,128)} fusion(f32[4096]{0:T(1024)S(1)} %bitcast.139, f32[144]{0:T(256)S(1)} %add_rsqrt_fusion, bf16[2,144,4096]{2,1,0:T(8,128)(2,1)} %param.10, bf16[144,64]{0,1:T(8,128)(2,1)S(1)} %fusion.30, bf16[144,64]{0,1:T(8,128)(2,1)S(1)} %fusion.29), kind=kOutput, calls=%fused_computation.20 | convolution fusion | flops 153427968 | bytes 3330624 | tf_op jit(solution)/shard_map/dot_general | solution.py:78
  20.5 3.5 %fusion.19 = f32[4096,128]{1,0:T(8,128)} fusion(f32[4096]{0:T(1024)S(1)} %bitcast.138, f32[144]{0:T(256)S(1)} %add_rsqrt_fusion.1, bf16[2,144,4096]{2,1,0:T(8,128)(2,1)} %param.10, bf16[144,64]{0,1:T(8,128)(2,1)S(1)} %fusion.28, bf16[144,64]{0,1:T(8,128)(2,1)S(1)} %fusion.27), kind=kOutput, calls=%fused_computation.21 | convolution fusion | flops 153427968 | bytes 3330624 | tf_op jit(solution)/shard_map/dot_general | solution.py:78
  24.1 34.8 %reduce-scatter.5.cloned.1.call-done = f32[512,128]{1,0:T(8,128)} async-done(((f32[4096,128]{1,0:T(8,128)}), f32[512,128]{1,0:T(8,128)}) %reduce-scatter.5.cloned.1.call-update) | async-done | bytes 262160 | tf_op jit(solution)/shard_map/reduce_scatter | solution.py:77
  58.8 36.9 %reduce-scatter.3.cloned.1.call-done = f32[512,128]{1,0:T(8,128)} async-done(((f32[4096,128]{1,0:T(8,128)}), f32[512,128]{1,0:T(8,128)}) %reduce-scatter.3.cloned.1.call-update) | async-done | bytes 262160 | tf_op jit(solution)/shard_map/reduce_scatter | solution.py:77
  97.1 45.8 %all-reduce.3.cloned.1.call-done = (f32[512,128]{1,0:T(8,128)}, f32[512,128]{1,0:T(8,128)}) async-done(((f32[512,128]{1,0:T(8,128)}, f32[512,128]{1,0:T(8,128)}), (f32[512,128]{1,0:T(8,128)}, f32[512,128]{1,0:T(8,128)})) %all-reduce.3.cloned.1.call-update) | async-done | bytes 524304 | tf_op jit(solution)/shard_map/psum | solution.py:85
  147.3 1.6 collective-permute-start.1
  148.9 1.3 compare_convert_fusion
  150.2 3.1 %collective-permute-done.1 = f32[2,2,64,64]{2,3,1,0:T(8,128)S(1)} collective-permute-done((f32[2,2,64,64]{2,3,1,0:T(8,128)S(1)}, f32[2,2,64,64]{2,3,1,0:T(8,128)S(1)}, u32[]{:S(2)}, u32[]{:S(2)}) %collective-permute-start.1) | collective-permute-done | bytes 65568 | tf_op jit(solution)/shard_map/ppermute | solution.py:94
  153.3 2.5 %collective-permute-start.2 = (f32[2,2,64,64]{2,3,1,0:T(8,128)S(1)}, f32[2,2,64,64]{2,3,1,0:T(8,128)S(1)}, u32[]{:S(2)}, u32[]{:S(2)}) collective-permute-start(f32[2,2,64,64]{2,3,1,0:T(8,128)S(1)} %fusion.82), channel_id=1, source_target_pairs={{0,4},{1,5},{2,6},{3,7},{4,0},{5,1},{6,2},{7,3},{8,12},{9,13},{10,... | collective-permute-start | bytes 196616 | tf_op jit(solution)/shard_map/ppermute | solution.py:94
  155.8 14.8 %collective-permute-done.2 = f32[2,2,64,64]{2,3,1,0:T(8,128)S(1)} collective-permute-done((f32[2,2,64,64]{2,3,1,0:T(8,128)S(1)}, f32[2,2,64,64]{2,3,1,0:T(8,128)S(1)}, u32[]{:S(2)}, u32[]{:S(2)}) %collective-permute-start.2) | collective-permute-done | bytes 65568 | tf_op jit(solution)/shard_map/ppermute | solution.py:94
  170.7 5.8 %cholesky.107 = f32[64,64]{1,0:T(8,128)S(1)} custom-call(f32[64,64]{1,0:T(8,128)S(1)} %fusion.62), custom_call_target="Cholesky" | custom-call | tf_op jit(solution)/shard_map/jit(cholesky)/cholesky | solution.py:57
  177.9 4.9 %custom-call.11 = f32[1,64,64]{1,2,0:T(8,128)S(1)} custom-call(f32[1,64,64]{2,1,0:T(8,128)S(1)} %fusion.56), custom_call_target="InvertDiagBlocksLowerTriangular" | custom-call | tf_op jit(solution)/shard_map/triangular_solve/custom-call.0 | solution.py:59
  182.9 5.8 %cholesky.96 = f32[64,64]{1,0:T(8,128)S(1)} custom-call(f32[64,64]{1,0:T(8,128)S(1)} %fusion.64), custom_call_target="Cholesky" | custom-call | tf_op jit(solution)/shard_map/jit(cholesky)/cholesky | solution.py:57
  190.1 4.9 %custom-call.10 = f32[1,64,64]{1,2,0:T(8,128)S(1)} custom-call(f32[1,64,64]{2,1,0:T(8,128)S(1)} %fusion.55), custom_call_target="InvertDiagBlocksLowerTriangular" | custom-call | tf_op jit(solution)/shard_map/triangular_solve/custom-call.0 | solution.py:59
  195.1 5.8 %cholesky.85 = f32[64,64]{1,0:T(8,128)S(1)} custom-call(f32[64,64]{1,0:T(8,128)S(1)} %fusion.66), custom_call_target="Cholesky" | custom-call | tf_op jit(solution)/shard_map/jit(cholesky)/cholesky | solution.py:57
  202.3 4.9 %custom-call.9 = f32[1,64,64]{1,2,0:T(8,128)S(1)} custom-call(f32[1,64,64]{2,1,0:T(8,128)S(1)} %fusion.54), custom_call_target="InvertDiagBlocksLowerTriangular" | custom-call | tf_op jit(solution)/shard_map/triangular_solve/custom-call.0 | solution.py:59
  207.3 5.8 %cholesky.74 = f32[64,64]{1,0:T(8,128)S(1)} custom-call(f32[64,64]{1,0:T(8,128)S(1)} %fusion.68), custom_call_target="Cholesky" | custom-call | tf_op jit(solution)/shard_map/jit(cholesky)/cholesky | solution.py:57
  214.5 4.9 %custom-call.8 = f32[1,64,64]{1,2,0:T(8,128)S(1)} custom-call(f32[1,64,64]{2,1,0:T(8,128)S(1)} %fusion.53), custom_call_target="InvertDiagBlocksLowerTriangular" | custom-call | tf_op jit(solution)/shard_map/triangular_solve/custom-call.0 | solution.py:59
  222.4 9.1 %all-gather.3.cloned.1.call-done = bf16[1,4096,1024]{2,1,0:T(8,128)(2,1)} async-done(((bf16[1,512,1024]{2,1,0:T(8,128)(2,1)}), bf16[1,4096,1024]{2,1,0:T(8,128)(2,1)}) %all-gather.3.cloned.1.call-update) | async-done | bytes 8388624 | tf_op jit(solution)/shard_map/all_gather | solution.py:106
  231.5 6.9 %fusion.13 = (f32[144]{0:T(256)S(1)}, f32[144,4096]{1,0:T(8,128)S(1)}) fusion(f32[144]{0:T(256)S(1)} %bitcast.141, bf16[2,144,4096]{2,1,0:T(8,128)(2,1)} %param.10, s32[]{:T(128)S(6)} %select_n.69, f32[4096]{0:T(1024)S(1)} %bitcast.140, bf16[1,4096,1024]{2,1,0:T(8,128)(2,1)} %all-gather.3.cloned.1.call-done, bf16[2,144,1024]{2,1,0:T(8,128)(2,1)S(1)} %copy-done.4), kind=kOutput, calls=%fused_computation.16 | convolution fusion | flops 1210908544 | bytes 12241472 | tf_op jit(solution)/shard_map/dot_general | solution.py:104
  238.4 1.6 fusion.16
  (74 shorter events, 17.9 us)
Async XLA Ops:
  7.2 88.8 %copy-start = (bf16[2,512,1024]{2,1,0:T(8,128)(2,1)S(1)}, bf16[2,512,1024]{2,1,0:T(8,128)(2,1)}, u32[]{:S(2)}) copy-start(bf16[2,512,1024]{2,1,0:T(8,128)(2,1)} %param.12) | copy-start | bytes 6291460
  7.2 6.9 %copy-start.6 = (s32[2]{0:T(128)S(1)}, s32[2]{0:T(128)}, u32[]{:S(2)}) copy-start(s32[2]{0:T(128)} %param.16) | copy-start | bytes 28
  7.2 9.2 %copy-start.5 = (f32[2,4096]{1,0:T(2,128)S(1)}, f32[2,4096]{1,0:T(2,128)}, u32[]{:S(2)}) copy-start(f32[2,4096]{1,0:T(2,128)} %param.13) | copy-start | bytes 98308
  7.2 51.6 %reduce-scatter.5.cloned.1.call-start = ((), (), s32[]{:S(2)}) async-start(), calls=%async_computation.3 | async-start | bytes 2359296 | tf_op jit(solution)/shard_map/reduce_scatter | solution.py:77
  20.0 75.8 %reduce-scatter.3.cloned.1.call-start = ((), (), s32[]{:S(2)}) async-start(), calls=%async_computation.2 | async-start | bytes 2359296 | tf_op jit(solution)/shard_map/reduce_scatter | solution.py:77
  24.0 118.8 %all-reduce.3.cloned.1.call-start = ((), (), s32[]{:S(2)}) async-start(), calls=%async_computation.5 | async-start | bytes 1048576 | tf_op jit(solution)/shard_map/psum | solution.py:85
  95.8 135.7 %all-gather.3.cloned.1.call-start = ((), (), s32[]{:S(2)}) async-start(), calls=%async_computation.4 | async-start | bytes 9437184 | tf_op jit(solution)/shard_map/all_gather | solution.py:106
  143.9 75.5 %copy-start.3 = (f32[512,128]{1,0:T(8,128)S(1)}, f32[512,128]{1,0:T(8,128)}, u32[]{:S(2)}) copy-start(f32[512,128]{1,0:T(8,128)} %get-tuple-element.10) | copy-start | bytes 786436
  145.4 74.9 %copy-start.2 = (f32[512,128]{1,0:T(8,128)S(1)}, f32[512,128]{1,0:T(8,128)}, u32[]{:S(2)}) copy-start(f32[512,128]{1,0:T(8,128)} %get-tuple-element.11) | copy-start | bytes 786436
  145.9 1.4 collective-permute-start
  147.3 5.9 %collective-permute-start.1 = (f32[2,2,64,64]{2,3,1,0:T(8,128)S(1)}, f32[2,2,64,64]{2,3,1,0:T(8,128)S(1)}, u32[]{:S(2)}, u32[]{:S(2)}) collective-permute-start(f32[2,2,64,64]{2,3,1,0:T(8,128)S(1)} %fusion.75), channel_id=1, source_target_pairs={{0,2},{1,3},{2,0},{3,1},{4,6},{5,7},{6,4},{7,5},{8,10},{9,11},{10,... | collective-permute-start | bytes 196616 | tf_op jit(solution)/shard_map/ppermute | solution.py:94
  153.3 17.3 %collective-permute-start.2 = (f32[2,2,64,64]{2,3,1,0:T(8,128)S(1)}, f32[2,2,64,64]{2,3,1,0:T(8,128)S(1)}, u32[]{:S(2)}, u32[]{:S(2)}) collective-permute-start(f32[2,2,64,64]{2,3,1,0:T(8,128)S(1)} %fusion.82), channel_id=1, source_target_pairs={{0,4},{1,5},{2,6},{3,7},{4,0},{5,1},{6,2},{7,3},{8,12},{9,13},{10,... | collective-permute-start | bytes 196616 | tf_op jit(solution)/shard_map/ppermute | solution.py:94
  219.4 12.1 %copy-start.4 = (bf16[2,144,1024]{2,1,0:T(8,128)(2,1)S(1)}, bf16[2,144,1024]{2,1,0:T(8,128)(2,1)}, u32[]{:S(2)}) copy-start(bf16[2,144,1024]{2,1,0:T(8,128)(2,1)} %param.11) | copy-start | bytes 1769476
  231.5 6.9 %copy-start.1 = (bf16[2,144,4096]{2,1,0:T(8,128)(2,1)S(1)}, bf16[2,144,4096]{2,1,0:T(8,128)(2,1)}, u32[]{:S(2)}) copy-start(bf16[2,144,4096]{2,1,0:T(8,128)(2,1)} %param.10) | copy-start | bytes 7077892
Sparse Core Ops, SparseCore 0:
  20.1 38.6 reduce-scatter.4
  61.1 34.5 reduce-scatter.2
  98.7 44.0 all-reduce.2
  144.9 86.5 all-gather.2
